TPU v7x, 32 devices: a whole 2x2x4 slice. The times are simulated.
32 devices in a mesh: row: 4 (over y, x), col: 8 (over z, core).
Axes of the slice: x: 2, y: 2, z: 4, core: 2. Of those that a mesh axis runs over, the one named last changes fastest.
Arguments:
- inputs: bfloat16 [2048, 25600], P('row', 'col'), may hold values from -6 to 6
- out_grads: bfloat16 [2048, 5120], P('col', 'row'), may hold values from -0.125 to 0.125
- weights: bfloat16 [5120, 25600], P('row', 'col'), may hold values from -3 to 3
- momentum: float32 [5120, 25600], P('row', 'col'), may hold values from -13 to 13
- right_factor: float32 [25600, 256], P('col'), may hold values from -6 to 6
Outputs:
- weights_new: float32 [5120, 25600], P('row', 'col')
- momentum_new: float32 [5120, 25600], P('row', 'col')
- factor_new: float32 [25600, 256], P('col')
All inputs are finite; a program needn't handle non-finite values.
Results may differ from a plain program's by a relative error of at most 0.0003.
Values may be sent and summed in bfloat16 or wider, within the bound.
No kernel may reach another device: no remote copies, remote signals or barrier semaphores. Data moves between devices by JAX's collectives and lax.ppermute only.
A program may use at most 128 MiB of HBM per device.

v0:
```python
import math
import jax
import jax.numpy as jnp
from jax import lax
from jax.sharding import PartitionSpec as P

M = 5120
N = 25600
RANK = 256
mix_rate = 0.95
step_rate = 0.3
weight_decay = 0.1
tiny_eps = 1e-06
highest = lax.Precision.HIGHEST


def inner_rows(left_side, right_in):
    return lax.dot_general(left_side, right_in, (((0,), (0,)), ((), ())), precision=highest)


def orthonormal(sketch_rows, gram_total):
    factor_low = jnp.linalg.cholesky(gram_total)
    return jax.scipy.linalg.solve_triangular(factor_low, sketch_rows.T, lower=True).T


def on_device(inputs, out_grads, weights, momentum, right_factor):
    grads_all = lax.all_gather(out_grads, "col", axis=0, tiled=True)
    gradient = lax.dot_general(
        grads_all,
        lax.all_gather(inputs, "row", axis=0, tiled=True),
        (((0,), (0,)), ((), ())),
        preferred_element_type=jnp.float32,
    )
    moment = momentum + gradient
    sketch_part = jnp.dot(moment, right_factor, precision=highest)
    sketch_rows = lax.psum(sketch_part, "col")
    gram_total = lax.psum(inner_rows(sketch_rows, sketch_rows), "row")
    basis_rows = orthonormal(sketch_rows, gram_total)
    right_part = inner_rows(moment, basis_rows)
    right_share = lax.psum_scatter(right_part, "row", scatter_dimension=0, tiled=True)
    squares = lax.psum(jnp.sum(right_share * right_share, axis=0), ("row", "col"))
    right_side = lax.all_gather(right_share, "row", axis=0, tiled=True)
    column_scale = lax.rsqrt(squares / N + tiny_eps)
    factor_new = right_side * column_scale
    momentum_new = moment - (1.0 - mix_rate) * jnp.dot(basis_rows, right_side.T, precision=highest)
    update = jnp.dot(basis_rows, factor_new.T, precision=highest)
    weights_new = (
        weights.astype(jnp.float32) * (1.0 - step_rate * weight_decay)
        - step_rate * math.sqrt(M / RANK) * update
    )
    return (weights_new, momentum_new, factor_new)


def solution(mesh):
    placed = (P("row", "col"), P("col", "row"), P("row", "col"), P("row", "col"), P("col", None))
    return jax.shard_map(
        on_device,
        mesh=mesh,
        in_specs=placed,
        out_specs=(P("row", "col"), P("row", "col"), P("col", None)),
        check_vma=False,
    )
```

profile of v0, /device:TPU:0, one launch (start us, length us, event | category | flops | bytes accessed | tf_op | source)
XLA Modules:
  0.0 616.2 jit_solution(3706774686516627048)
XLA Ops:
  7.2 0.0 copy-start
  7.2 0.0 all-gather.4.cloned.1.call-start
  7.2 0.7 all-gather.4.cloned.1.call-update
  7.9 0.0 all-gather.6.cloned.1.call-start
  8.0 0.7 all-gather.6.cloned.1.call-update
  8.7 0.0 all-reduce.4.cloned.1.call-start
  8.7 59.7 %all-gather.4.cloned.1.call-done = bf16[2048,1280]{1,0:T(8,128)(2,1)} async-done(((bf16[256,1280]{1,0:T(8,128)(2,1)}), bf16[2048,1280]{1,0:T(8,128)(2,1)}) %all-gather.4.cloned.1.call-update) | async-done | bytes 5242896 | tf_op jit(solution)/shard_map/all_gather | solution.py:27
  68.4 127.4 %all-gather.6.cloned.1.call-done = bf16[2048,3200]{1,0:T(8,128)(2,1)} async-done(((bf16[512,3200]{1,0:T(8,128)(2,1)}), bf16[2048,3200]{1,0:T(8,128)(2,1)}) %all-gather.6.cloned.1.call-update) | async-done | bytes 13107216 | tf_op jit(solution)/shard_map/all_gather | solution.py:30
  195.8 29.4 %convolution_add_fusion = f32[1280,3200]{1,0:T(8,128)} fusion(f32[1280,3200]{1,0:T(8,128)} %param.8, bf16[2048,1280]{1,0:T(8,128)(2,1)} %all-gather.4.cloned.1.call-done, bf16[2048,3200]{1,0:T(8,128)(2,1)} %all-gather.6.cloned.1.call-done), kind=kOutput, calls=%fused_computation.2 | convolution fusion | flops 16781312000 | bytes 51118080 | tf_op jit(solution)/shard_map/dot_general | solution.py:28
  225.1 17.8 %fusion.15 = f32[1280,256]{1,0:T(8,128)} fusion(f32[1280,3200]{1,0:T(8,128)} %convolution_add_fusion, f32[3200,256]{1,0:T(8,128)S(1)} %copy-done), kind=kOutput, calls=%fused_computation.41 | convolution fusion | flops 12582912000 | bytes 20971520 | tf_op jit(solution)/shard_map/dot_general | solution.py:35
  242.9 0.0 all-reduce.4.cloned.1.call-update
  242.9 0.0 all-reduce.6.cloned.1.call-start
  243.0 60.5 %all-reduce.4.cloned.1.call-done = f32[1280,256]{1,0:T(8,128)} async-done(((f32[1280,256]{1,0:T(8,128)}), f32[1280,256]{1,0:T(8,128)}) %all-reduce.4.cloned.1.call-update) | async-done | bytes 1310736 | tf_op jit(solution)/shard_map/psum | solution.py:36
  303.5 4.8 fusion.16
  308.3 0.0 all-reduce.6.cloned.1.call-update
  308.4 0.2 reduce-scatter.2.cloned.1.call-start
  308.6 42.0 %all-reduce.6.cloned.1.call-done = f32[256,256]{0,1:T(8,128)} async-done(((f32[256,256]{0,1:T(8,128)}), f32[256,256]{0,1:T(8,128)}) %all-reduce.6.cloned.1.call-update) | async-done | bytes 262160 | tf_op jit(solution)/shard_map/psum | solution.py:37
  350.6 1.1 copy.9
  351.7 1.0 fusion.5
  352.7 11.7 %cholesky.50 = f32[128,128]{1,0:T(8,128)S(1)} custom-call(f32[128,128]{1,0:T(8,128)S(1)} %cholesky.118), custom_call_target="Cholesky" | custom-call | tf_op jit(solution)/shard_map/jit(cholesky)/cholesky | solution.py:22
  364.4 9.8 %custom-call.15 = f32[1,128,128]{1,2,0:T(8,128)S(1)} custom-call(f32[1,128,128]{2,1,0:T(8,128)S(1)} %get-tuple-element.24), custom_call_target="InvertDiagBlocksLowerTriangular" | custom-call | tf_op jit(solution)/shard_map/jit(cholesky)/cholesky | solution.py:22
  374.3 0.2 constant_dynamic-update-slice_fusion.1
  374.5 0.3 convolution_subtract_fusion.1
  374.8 11.7 %cholesky.105 = f32[128,128]{1,0:T(8,128)S(1)} custom-call(f32[128,128]{1,0:T(8,128)S(1)} %convolution_subtract_fusion.1), custom_call_target="Cholesky" | custom-call | tf_op jit(solution)/shard_map/jit(cholesky)/cholesky | solution.py:22
  386.5 0.7 compare_reduce_fusion
  388.6 0.1 triangular_solve.57
  388.6 4.2 while.1
  388.8 0.6 fusion.31
  389.4 1.4 bitcast_dynamic-update-slice_fusion.2
  390.8 0.6 fusion.31
  391.4 1.4 bitcast_dynamic-update-slice_fusion.2
  392.8 19.7 %custom-call.16 = f32[2,128,128]{1,2,0:T(8,128)S(1)} custom-call(f32[2,128,128]{2,1,0:T(8,128)S(1)} %get-tuple-element.10), custom_call_target="InvertDiagBlocksLowerTriangular" | custom-call | tf_op jit(solution)/shard_map/jit(_solve_triangular)/triangular_solve | solution.py:23
  412.5 0.8 fusion.3
  413.3 1.2 convolution_subtract_fusion
  414.5 0.8 fusion.7
  415.2 0.0 copy-start.6
  415.2 32.1 %fusion.2 = f32[3200,256]{1,0:T(8,128)} fusion(f32[1280,3200]{1,0:T(8,128)} %convolution_add_fusion, f32[128,1280]{1,0:T(8,128)S(1)} %fusion.7, f32[128,1280]{1,0:T(8,128)S(1)} %fusion.3), kind=kOutput, calls=%fused_computation.11 | convolution fusion | flops 12583239680 | bytes 20971520 | tf_op jit(solution)/shard_map/dot_general | solution.py:18
  447.4 0.0 reduce-scatter.2.cloned.1.call-update
  447.4 0.0 all-gather.8.cloned.1.call-start
  447.4 45.1 %reduce-scatter.2.cloned.1.call-done = f32[800,256]{1,0:T(8,128)} async-done(((f32[3200,256]{1,0:T(8,128)}), f32[800,256]{1,0:T(8,128)}) %reduce-scatter.2.cloned.1.call-update) | async-done | bytes 819216 | tf_op jit(solution)/shard_map/reduce_scatter | solution.py:40
  492.5 0.0 all-gather.8.cloned.1.call-update
  492.6 1.3 multiply_reduce_fusion
  493.8 40.3 %psum.23 = f32[256]{0:T(256)S(1)} all-reduce(f32[256]{0:T(256)S(1)} %multiply_reduce_fusion), channel_id=1, replica_groups=mesh['row'=4,'col'=8] {'row','col'}, use_global_device_ids=true, to_apply=%region_8.9 | all-reduce | flops 256 | bytes 2048 | tf_op jit(solution)/shard_map/psum | solution.py:41
  534.1 6.0 all-gather.8.cloned.1.call-done
  540.1 2.1 broadcast_multiply_fusion
  542.2 0.0 copy-start.3
  542.3 32.8 %fusion.1 = f32[1280,3200]{1,0:T(8,128)} fusion(f32[3200,256]{1,0:T(8,128)S(1)} %broadcast_multiply_fusion, bf16[1280,3200]{1,0:T(8,128)(2,1)} %param.7, f32[128,1280]{1,0:T(8,128)S(1)} %fusion.7, f32[128,1280]{1,0:T(8,128)S(1)} %fusion.3), kind=kOutput, calls=%fused_computation.6 | convolution fusion | flops 12599623680 | bytes 29163520 | tf_op jit(solution)/shard_map/dot_general | solution.py:46
  575.0 34.1 %fusion = f32[1280,3200]{1,0:T(8,128)} fusion(f32[1280,3200]{1,0:T(8,128)} %convolution_add_fusion, f32[3200,256]{1,0:T(8,128)S(1)} %copy-done.4, f32[128,1280]{1,0:T(8,128)} %copy-done.6, f32[128,1280]{1,0:T(8,128)} %copy-done.2), kind=kOutput, calls=%fused_computation.4 | convolution fusion | flops 12591431680 | bytes 37355520 | tf_op jit(solution)/shard_map/dot_general | solution.py:45
  (21 shorter events, 0.2 us)
Async XLA Ops:
  7.2 217.9 %copy-start = (f32[3200,256]{1,0:T(8,128)S(1)}, f32[3200,256]{1,0:T(8,128)}, u32[]{:S(2)}) copy-start(f32[3200,256]{1,0:T(8,128)} %param.9) | copy-start | bytes 9830404
  7.2 61.2 %all-gather.4.cloned.1.call-start = ((), (), s32[]{:S(2)}) async-start(), calls=%async_computation.1 | async-start | bytes 5898240 | tf_op jit(solution)/shard_map/all_gather | solution.py:27
  7.9 187.8 %all-gather.6.cloned.1.call-start = ((), (), s32[]{:S(2)}) async-start(), calls=%async_computation.2 | async-start | bytes 16384000 | tf_op jit(solution)/shard_map/all_gather | solution.py:30
  8.7 294.8 %all-reduce.4.cloned.1.call-start = ((), (), s32[]{:S(2)}) async-start(), calls=%async_computation.3 | async-start | bytes 2621440 | tf_op jit(solution)/shard_map/psum | solution.py:36
  242.9 107.7 %all-reduce.6.cloned.1.call-start = ((), (), s32[]{:S(2)}) async-start(), calls=%async_computation.4 | async-start | bytes 524288 | tf_op jit(solution)/shard_map/psum | solution.py:37
  303.5 109.0 %copy-start.5 = (f32[1280,256]{1,0:T(8,128)S(1)}, f32[1280,256]{1,0:T(8,128)}, u32[]{:S(2)}) copy-start(f32[1280,256]{1,0:T(8,128)} %all-reduce.4.cloned.1.call-done) | copy-start | bytes 3932164
  308.4 184.2 %reduce-scatter.2.cloned.1.call-start = ((), (), s32[]{:S(2)}) async-start(), calls=%async_computation.5 | async-start | bytes 4096000 | tf_op jit(solution)/shard_map/reduce_scatter | solution.py:40
  413.3 129.0 %copy-start.2 = (f32[128,1280]{1,0:T(8,128)}, f32[128,1280]{1,0:T(8,128)S(1)}, u32[]{:S(2)}) copy-start(f32[128,1280]{1,0:T(8,128)S(1)} %fusion.3) | copy-start | bytes 1966084
  415.2 127.0 %copy-start.6 = (f32[128,1280]{1,0:T(8,128)}, f32[128,1280]{1,0:T(8,128)S(1)}, u32[]{:S(2)}) copy-start(f32[128,1280]{1,0:T(8,128)S(1)} %fusion.7) | copy-start | bytes 1966084
  447.4 92.7 %all-gather.8.cloned.1.call-start = ((), (), s32[]{:S(2)}) async-start(), calls=%async_computation.6 | async-start | bytes 4096000 | tf_op jit(solution)/shard_map/all_gather | solution.py:42
  542.2 32.8 %copy-start.3 = (f32[3200,256]{1,0:T(8,128)}, f32[3200,256]{1,0:T(8,128)S(1)}, u32[]{:S(2)}) copy-start(f32[3200,256]{1,0:T(8,128)S(1)} %broadcast_multiply_fusion) | copy-start | bytes 9830404
  542.3 32.8 %copy-start.4 = (f32[3200,256]{1,0:T(8,128)S(1)}, f32[3200,256]{1,0:T(8,128)}, u32[]{:S(2)}) copy-start(f32[3200,256]{1,0:T(8,128)} %all-gather.8.cloned.1.call-done) | copy-start | bytes 9830404
  575.0 34.1 %copy-start.1 = (f32[3200,256]{1,0:T(8,128)S(1)}, f32[3200,256]{1,0:T(8,128)}, u32[]{:S(2)}) copy-start(f32[3200,256]{1,0:T(8,128)} %param.9) | copy-start | bytes 9830404
Sparse Core Ops, SparseCore 0:
  9.6 58.6 all-gather.3
  70.2 125.5 all-gather.5
  243.0 60.4 all-reduce.3
  308.5 42.0 all-reduce.5
  447.5 44.9 reduce-scatter.1
  494.2 45.7 all-gather.7
where the time goes:
time: 623 us; the launch traced here: 616 us
  waiting for transfers between devices  342 us (55%)
  matrix products  154 us (25%)
  other arithmetic  58.1 us (9%)
  blocking collectives  40.3 us (6%)
  between operations  15.8 us (3%)
    all_gather x1, waiting for transfers between devices, on_device(): lax.all_gather(inputs, 'row', axis=0, tiled=True)  127 us
    psum x1, waiting for transfers between devices, on_device(): sketch_rows = lax.psum(sketch_part, 'col')  60.5 us
    all_gather x1, waiting for transfers between devices, on_device(): grads_all = lax.all_gather(out_grads, 'col', axis=0, tiled=True)  59.7 us
    reduce_scatter x1, waiting for transfers between devices, on_device(): lax.psum_scatter(right_part, 'row', scatter_dimension=0, tiled=True)  45.1 us
    psum x1, waiting for transfers between devices, on_device(): gram_total = lax.psum(inner_rows(sketch_rows, sketch_rows), 'row')  42 us
    psum x1, blocking collectives, on_device(): lax.psum(jnp.sum(right_share * right_share, axis=0), ('row', 'col'))  40.3 us
    dot_general x2, matrix products, inner_rows(): lax.dot_general(left_side, right_in, (((0,), (0,)), ((), ())), precision=...  36.9 us
    dot_general x1, matrix products, on_device(): jnp.dot(basis_rows, right_side.T, precision=highest)  34.1 us
  transfers between devices with their start and end apart: 6, of which 6 were waited for; matrix products, arithmetic and copies ran while one was open for 0% of the time, Pallas kernels for 0%

commit v1 on v0

--- a/solution.py
+++ b/solution.py
@@ -38,7 +38,7 @@
     basis_rows = orthonormal(sketch_rows, gram_total)
     right_part = inner_rows(moment, basis_rows)
     right_share = lax.psum_scatter(right_part, "row", scatter_dimension=0, tiled=True)
-    squares = lax.psum(jnp.sum(right_share * right_share, axis=0), ("row", "col"))
+    squares = lax.psum(lax.psum(jnp.sum(right_share * right_share, axis=0), "col"), "row")
     right_side = lax.all_gather(right_share, "row", axis=0, tiled=True)
     column_scale = lax.rsqrt(squares / N + tiny_eps)
     factor_new = right_side * column_scale

time: 623 us -> 623 us (level)
  blocking collectives: 40.3 us -> 25.1 us
  waiting for transfers between devices: 342 us -> 356 us
    psum x1 -> x2, blocking collectives: 40.3 us -> 25.1 us  [the longest x1 16.2 us: on_device(): lax.psum(jnp.sum(right_share * right_share, axis=0), 'col')]
    all_gather x1, waiting for transfers between devices: 5.98 us -> 20.3 us  [on_device(): right_side = lax.all_gather(right_share, 'row', axis=0, tiled=True)]
where the time goes in v1:
time: 623 us; the launch traced here: 616 us
  waiting for transfers between devices  356 us (57%)
  matrix products  154 us (25%)
  other arithmetic  58.1 us (9%)
  blocking collectives  25.1 us (4%)
  between operations  15.8 us (3%)
    all_gather x1, waiting for transfers between devices, on_device(): lax.all_gather(inputs, 'row', axis=0, tiled=True)  127 us
    psum x1, waiting for transfers between devices, on_device(): sketch_rows = lax.psum(sketch_part, 'col')  60.5 us
    all_gather x1, waiting for transfers between devices, on_device(): grads_all = lax.all_gather(out_grads, 'col', axis=0, tiled=True)  59.7 us
    reduce_scatter x1, waiting for transfers between devices, on_device(): lax.psum_scatter(right_part, 'row', scatter_dimension=0, tiled=True)  45.1 us
    psum x1, waiting for transfers between devices, on_device(): gram_total = lax.psum(inner_rows(sketch_rows, sketch_rows), 'row')  42 us
    dot_general x2, matrix products, inner_rows(): lax.dot_general(left_side, right_in, (((0,), (0,)), ((), ())), precision=...  36.9 us
    dot_general x1, matrix products, on_device(): jnp.dot(basis_rows, right_side.T, precision=highest)  34.1 us
    another operation x6, other arithmetic, orthonormal(): factor_low = jnp.linalg.cholesky(gram_total)  34 us
  transfers between devices with their start and end apart: 6, of which 6 were waited for; matrix products, arithmetic and copies ran while one was open for 0% of the time, Pallas kernels for 0%

profile of v1, /device:TPU:0, one launch (start us, length us, event | category | flops | bytes accessed | tf_op | source)
XLA Modules:
  0.0 615.5 jit_solution(6904370140503912813)
XLA Ops:
  7.2 0.0 copy-start
  7.2 0.0 all-gather.4.cloned.1.call-start
  7.2 0.7 all-gather.4.cloned.1.call-update
  7.9 0.0 all-gather.6.cloned.1.call-start
  8.0 0.7 all-gather.6.cloned.1.call-update
  8.7 0.0 all-reduce.4.cloned.1.call-start
  8.7 59.7 %all-gather.4.cloned.1.call-done = bf16[2048,1280]{1,0:T(8,128)(2,1)} async-done(((bf16[256,1280]{1,0:T(8,128)(2,1)}), bf16[2048,1280]{1,0:T(8,128)(2,1)}) %all-gather.4.cloned.1.call-update) | async-done | bytes 5242896 | tf_op jit(solution)/shard_map/all_gather | solution.py:27
  68.4 127.4 %all-gather.6.cloned.1.call-done = bf16[2048,3200]{1,0:T(8,128)(2,1)} async-done(((bf16[512,3200]{1,0:T(8,128)(2,1)}), bf16[2048,3200]{1,0:T(8,128)(2,1)}) %all-gather.6.cloned.1.call-update) | async-done | bytes 13107216 | tf_op jit(solution)/shard_map/all_gather | solution.py:30
  195.8 29.4 %convolution_add_fusion = f32[1280,3200]{1,0:T(8,128)} fusion(f32[1280,3200]{1,0:T(8,128)} %param.8, bf16[2048,1280]{1,0:T(8,128)(2,1)} %all-gather.4.cloned.1.call-done, bf16[2048,3200]{1,0:T(8,128)(2,1)} %all-gather.6.cloned.1.call-done), kind=kOutput, calls=%fused_computation.2 | convolution fusion | flops 16781312000 | bytes 51118080 | tf_op jit(solution)/shard_map/dot_general | solution.py:28
  225.1 17.8 %fusion.15 = f32[1280,256]{1,0:T(8,128)} fusion(f32[1280,3200]{1,0:T(8,128)} %convolution_add_fusion, f32[3200,256]{1,0:T(8,128)S(1)} %copy-done), kind=kOutput, calls=%fused_computation.41 | convolution fusion | flops 12582912000 | bytes 20971520 | tf_op jit(solution)/shard_map/dot_general | solution.py:35
  242.9 0.0 all-reduce.4.cloned.1.call-update
  242.9 0.0 all-reduce.6.cloned.1.call-start
  243.0 60.5 %all-reduce.4.cloned.1.call-done = f32[1280,256]{1,0:T(8,128)} async-done(((f32[1280,256]{1,0:T(8,128)}), f32[1280,256]{1,0:T(8,128)}) %all-reduce.4.cloned.1.call-update) | async-done | bytes 1310736 | tf_op jit(solution)/shard_map/psum | solution.py:36
  303.5 4.8 fusion.16
  308.3 0.0 all-reduce.6.cloned.1.call-update
  308.4 0.2 reduce-scatter.2.cloned.1.call-start
  308.6 42.0 %all-reduce.6.cloned.1.call-done = f32[256,256]{0,1:T(8,128)} async-done(((f32[256,256]{0,1:T(8,128)}), f32[256,256]{0,1:T(8,128)}) %all-reduce.6.cloned.1.call-update) | async-done | bytes 262160 | tf_op jit(solution)/shard_map/psum | solution.py:37
  350.6 1.1 copy.9
  351.7 1.0 fusion.5
  352.7 11.7 %cholesky.50 = f32[128,128]{1,0:T(8,128)S(1)} custom-call(f32[128,128]{1,0:T(8,128)S(1)} %cholesky.118), custom_call_target="Cholesky" | custom-call | tf_op jit(solution)/shard_map/jit(cholesky)/cholesky | solution.py:22
  364.4 9.8 %custom-call.15 = f32[1,128,128]{1,2,0:T(8,128)S(1)} custom-call(f32[1,128,128]{2,1,0:T(8,128)S(1)} %get-tuple-element.24), custom_call_target="InvertDiagBlocksLowerTriangular" | custom-call | tf_op jit(solution)/shard_map/jit(cholesky)/cholesky | solution.py:22
  374.3 0.2 constant_dynamic-update-slice_fusion.1
  374.5 0.3 convolution_subtract_fusion.1
  374.8 11.7 %cholesky.105 = f32[128,128]{1,0:T(8,128)S(1)} custom-call(f32[128,128]{1,0:T(8,128)S(1)} %convolution_subtract_fusion.1), custom_call_target="Cholesky" | custom-call | tf_op jit(solution)/shard_map/jit(cholesky)/cholesky | solution.py:22
  386.5 0.7 compare_reduce_fusion
  388.6 0.1 triangular_solve.57
  388.7 4.3 while.1
  388.9 0.6 fusion.31
  389.5 1.4 bitcast_dynamic-update-slice_fusion.2
  390.9 0.6 fusion.31
  391.5 1.4 bitcast_dynamic-update-slice_fusion.2
  392.9 19.7 %custom-call.16 = f32[2,128,128]{1,2,0:T(8,128)S(1)} custom-call(f32[2,128,128]{2,1,0:T(8,128)S(1)} %get-tuple-element.10), custom_call_target="InvertDiagBlocksLowerTriangular" | custom-call | tf_op jit(solution)/shard_map/jit(_solve_triangular)/triangular_solve | solution.py:23
  412.6 0.8 fusion.3
  413.4 1.2 convolution_subtract_fusion
  414.6 0.8 fusion.7
  415.4 32.1 %fusion.2 = f32[3200,256]{1,0:T(8,128)} fusion(f32[1280,3200]{1,0:T(8,128)} %convolution_add_fusion, f32[128,1280]{1,0:T(8,128)S(1)} %fusion.7, f32[128,1280]{1,0:T(8,128)S(1)} %fusion.3), kind=kOutput, calls=%fused_computation.11 | convolution fusion | flops 12583239680 | bytes 20971520 | tf_op jit(solution)/shard_map/dot_general | solution.py:18
  447.5 0.0 reduce-scatter.2.cloned.1.call-update
  447.5 0.0 all-gather.8.cloned.1.call-start
  447.6 45.1 %reduce-scatter.2.cloned.1.call-done = f32[800,256]{1,0:T(8,128)} async-done(((f32[3200,256]{1,0:T(8,128)}), f32[800,256]{1,0:T(8,128)}) %reduce-scatter.2.cloned.1.call-update) | async-done | bytes 819216 | tf_op jit(solution)/shard_map/reduce_scatter | solution.py:40
  492.7 0.0 all-gather.8.cloned.1.call-update
  492.7 1.3 multiply_reduce_fusion
  494.0 16.2 %psum.30 = f32[256]{0:T(256)S(1)} all-reduce(f32[256]{0:T(256)S(1)} %multiply_reduce_fusion), channel_id=1, replica_groups=mesh['row'=4,'col'=8] {'col'}, use_global_device_ids=true, to_apply=%region_8.9 | all-reduce | flops 256 | bytes 2048 | tf_op jit(solution)/shard_map/psum | solution.py:41
  510.2 8.9 %psum.31 = f32[256]{0:T(256)S(1)} all-reduce(f32[256]{0:T(256)S(1)} %psum.30), channel_id=1, replica_groups=mesh['row'=4,'col'=8] {'row'}, use_global_device_ids=true, to_apply=%region_9.10 | all-reduce | flops 256 | bytes 2048 | tf_op jit(solution)/shard_map/psum | solution.py:41
  519.1 20.3 %all-gather.8.cloned.1.call-done = f32[3200,256]{1,0:T(8,128)} async-done(((f32[800,256]{1,0:T(8,128)}), f32[3200,256]{1,0:T(8,128)}) %all-gather.8.cloned.1.call-update) | async-done | bytes 3276816 | tf_op jit(solution)/shard_map/all_gather | solution.py:42
  539.4 2.1 broadcast_multiply_fusion
  541.6 0.0 copy-start.3
  541.6 32.8 %fusion.1 = f32[1280,3200]{1,0:T(8,128)} fusion(f32[3200,256]{1,0:T(8,128)S(1)} %broadcast_multiply_fusion, bf16[1280,3200]{1,0:T(8,128)(2,1)} %param.7, f32[128,1280]{1,0:T(8,128)S(1)} %fusion.7, f32[128,1280]{1,0:T(8,128)S(1)} %fusion.3), kind=kOutput, calls=%fused_computation.6 | convolution fusion | flops 12599623680 | bytes 29163520 | tf_op jit(solution)/shard_map/dot_general | solution.py:46
  574.4 34.1 %fusion = f32[1280,3200]{1,0:T(8,128)} fusion(f32[1280,3200]{1,0:T(8,128)} %convolution_add_fusion, f32[3200,256]{1,0:T(8,128)S(1)} %copy-done.4, f32[128,1280]{1,0:T(8,128)} %copy-done.6, f32[128,1280]{1,0:T(8,128)} %copy-done.2), kind=kOutput, calls=%fused_computation.4 | convolution fusion | flops 12591431680 | bytes 37355520 | tf_op jit(solution)/shard_map/dot_general | solution.py:45
  (22 shorter events, 0.2 us)
Async XLA Ops:
  7.2 217.9 %copy-start = (f32[3200,256]{1,0:T(8,128)S(1)}, f32[3200,256]{1,0:T(8,128)}, u32[]{:S(2)}) copy-start(f32[3200,256]{1,0:T(8,128)} %param.9) | copy-start | bytes 9830404
  7.2 61.2 %all-gather.4.cloned.1.call-start = ((), (), s32[]{:S(2)}) async-start(), calls=%async_computation.1 | async-start | bytes 5898240 | tf_op jit(solution)/shard_map/all_gather | solution.py:27
  7.9 187.8 %all-gather.6.cloned.1.call-start = ((), (), s32[]{:S(2)}) async-start(), calls=%async_computation.2 | async-start | bytes 16384000 | tf_op jit(solution)/shard_map/all_gather | solution.py:30
  8.7 294.8 %all-reduce.4.cloned.1.call-start = ((), (), s32[]{:S(2)}) async-start(), calls=%async_computation.3 | async-start | bytes 2621440 | tf_op jit(solution)/shard_map/psum | solution.py:36
  242.9 107.7 %all-reduce.6.cloned.1.call-start = ((), (), s32[]{:S(2)}) async-start(), calls=%async_computation.4 | async-start | bytes 524288 | tf_op jit(solution)/shard_map/psum | solution.py:37
  303.5 109.1 %copy-start.5 = (f32[1280,256]{1,0:T(8,128)S(1)}, f32[1280,256]{1,0:T(8,128)}, u32[]{:S(2)}) copy-start(f32[1280,256]{1,0:T(8,128)} %all-reduce.4.cloned.1.call-done) | copy-start | bytes 3932164
  308.4 184.3 %reduce-scatter.2.cloned.1.call-start = ((), (), s32[]{:S(2)}) async-start(), calls=%async_computation.5 | async-start | bytes 4096000 | tf_op jit(solution)/shard_map/reduce_scatter | solution.py:40
  413.4 128.2 %copy-start.2 = (f32[128,1280]{1,0:T(8,128)}, f32[128,1280]{1,0:T(8,128)S(1)}, u32[]{:S(2)}) copy-start(f32[128,1280]{1,0:T(8,128)S(1)} %fusion.3) | copy-start | bytes 1966084
  415.4 126.2 %copy-start.6 = (f32[128,1280]{1,0:T(8,128)}, f32[128,1280]{1,0:T(8,128)S(1)}, u32[]{:S(2)}) copy-start(f32[128,1280]{1,0:T(8,128)S(1)} %fusion.7) | copy-start | bytes 1966084
  447.5 91.9 %all-gather.8.cloned.1.call-start = ((), (), s32[]{:S(2)}) async-start(), calls=%async_computation.6 | async-start | bytes 4096000 | tf_op jit(solution)/shard_map/all_gather | solution.py:42
  541.6 32.8 %copy-start.3 = (f32[3200,256]{1,0:T(8,128)}, f32[3200,256]{1,0:T(8,128)S(1)}, u32[]{:S(2)}) copy-start(f32[3200,256]{1,0:T(8,128)S(1)} %broadcast_multiply_fusion) | copy-start | bytes 9830404
  541.6 32.8 %copy-start.4 = (f32[3200,256]{1,0:T(8,128)S(1)}, f32[3200,256]{1,0:T(8,128)}, u32[]{:S(2)}) copy-start(f32[3200,256]{1,0:T(8,128)} %all-gather.8.cloned.1.call-done) | copy-start | bytes 9830404
  574.4 34.1 %copy-start.1 = (f32[3200,256]{1,0:T(8,128)S(1)}, f32[3200,256]{1,0:T(8,128)}, u32[]{:S(2)}) copy-start(f32[3200,256]{1,0:T(8,128)} %param.9) | copy-start | bytes 9830404
Sparse Core Ops, SparseCore 0:
  9.6 58.6 all-gather.3
  70.2 125.5 all-gather.5
  243.0 60.4 all-reduce.3
  308.5 42.0 all-reduce.5
  447.6 44.9 reduce-scatter.1
  494.4 45.0 all-gather.7
